TPU v7x, 512 devices: a whole 4x8x8 slice. The times are simulated.
512 devices in a mesh: blk: 64 (over z_hi, y, core), rep: 8 (over z_lo, x).
Axes of the slice: x: 4, y: 8, z: 8 (z_hi: 4, z_lo: 2; z = z_hi * 2 + z_lo), core: 2. Of those that a mesh axis runs over, the one named last changes fastest.
Arguments:
- features: bfloat16 [32768, 128], P('blk'), may hold values from -6 to 6
- weight: bfloat16 [128, 256], replicated, may hold values from -0.5 to 0.5
- tile_vals: bfloat16 [64, 8, 8, 12, 128, 128], P('blk', 'rep'), may hold values from -0.0390625 to 0.0390625
- tile_pos: int32 [64, 8, 8, 12], P('blk', 'rep'), may hold values from 0 to 15, as said below
- tile_count: int32 [64, 8, 8], P('blk', 'rep'), may hold values from 1 to 12, as said below
- cotangent: bfloat16 [32768, 256], P(('blk', 'rep')), may hold values from -6 to 6
Outputs:
- activations: bfloat16 [32768, 256], P(('blk', 'rep'))
- feat_grad: bfloat16 [32768, 128], P(('blk', 'rep'))
- weight_grad: float32 [128, 256], replicated
Inputs may be any that keep to these rules, and one draw needn't show every extreme that they name: `tile_pos`: within one row group, copy and section the entries are distinct. `tile_count`: row group 0 has all 12 slots live in every copy and section.
All inputs are finite; a program needn't handle non-finite values.
Results may differ from a plain program's by a relative error of at most 0.014.
Values may be sent and summed in bfloat16 or wider, within the bound.
A program may use at most 128 MiB of HBM per device.

v0:
```python
import jax
import jax.numpy as jnp
from jax import lax
from jax.sharding import PartitionSpec as P


def gelu_tanh(value):
    return jax.nn.gelu(value, approximate=True)


def skewed(block, sign):
    blks, reps = (lax.axis_size("blk"), lax.axis_size("rep"))
    route = [
        (b * reps + r, (b + sign * r) % blks * reps + r) for b in range(blks) for r in range(reps)
    ]
    return lax.ppermute(block, ("blk", "rep"), route)


def split_dot(left, right):
    high = left.astype(jnp.bfloat16)
    low = (left - high.astype(jnp.float32)).astype(jnp.bfloat16)
    return jnp.dot(high, right, preferred_element_type=jnp.float32) + jnp.dot(
        low, right, preferred_element_type=jnp.float32
    )


def dense_adjacency(tiles, positions, counts, group, blocks):
    sections, slots = positions.shape
    cells = jnp.arange(blocks * blocks, dtype=jnp.int32)
    live = jnp.arange(slots, dtype=jnp.int32)[None, :] < counts[:, None]
    hits = (positions[:, None, :] == cells[None, :, None]) & live[:, None, :]
    slot_of = jnp.argmax(hits, axis=-1).astype(jnp.int32)
    filled = jnp.any(hits, axis=-1)
    order = (group - jnp.arange(sections, dtype=jnp.int32)) % sections
    slot_of, filled = (slot_of[order], filled[order])
    picked = tiles[order[:, None], slot_of]
    return jnp.where(filled[..., None, None], picked, jnp.zeros((), tiles.dtype)).reshape(
        sections, blocks, blocks, tiles.shape[-2], tiles.shape[-1]
    )


def local(features, weight, tile_vals, tile_pos, tile_count, cotangent):
    rep_size = lax.axis_size("rep")
    blk_size = lax.axis_size("blk")
    blk_index = lax.axis_index("blk")
    tile_size = tile_vals.shape[-1]
    rows, feat = features.shape
    blocks = rows // tile_size
    rings = [[r + k * rep_size for k in range(blk_size // rep_size)] for r in range(rep_size)]
    adjacency = dense_adjacency(
        tile_vals[0, 0], tile_pos[0, 0], tile_count[0, 0], blk_index // rep_size, blocks
    )
    gathered = lax.all_gather(skewed(features, 1), "blk", axis_index_groups=rings)
    columns = gathered.reshape(-1, blocks, tile_size, feat)
    mixed = jnp.einsum(
        "jnmik,jmkf->nif", adjacency, columns, preferred_element_type=jnp.float32
    ).reshape(rows, feat)
    mixed = lax.psum_scatter(mixed, "rep", scatter_dimension=0, tiled=True)
    pre = split_dot(mixed, weight)
    outputs, pullback = jax.vjp(gelu_tanh, pre)
    activations = outputs.astype(jnp.bfloat16)
    pre_grad = pullback(cotangent.astype(jnp.float32))[0].astype(jnp.bfloat16)
    weight_grad = lax.dot_general(
        mixed.astype(jnp.bfloat16),
        pre_grad,
        (((0,), (0,)), ((), ())),
        preferred_element_type=jnp.float32,
    )
    weight_grad = lax.psum(lax.psum(weight_grad, "rep"), "blk")
    row_grad = lax.dot_general(
        pre_grad, weight, (((1,), (1,)), ((), ())), preferred_element_type=jnp.float32
    ).astype(jnp.bfloat16)
    row_grad = lax.all_gather(row_grad, "rep", axis=0, tiled=True).reshape(blocks, tile_size, feat)
    partial = jnp.einsum(
        "jnmik,nif->jmkf", adjacency, row_grad, preferred_element_type=jnp.float32
    ).reshape(-1, rows, feat)
    partial = lax.psum_scatter(partial, "blk", scatter_dimension=0, axis_index_groups=rings)
    partial = skewed(partial, -1)
    feat_grad = lax.psum_scatter(partial, "rep", scatter_dimension=0, tiled=True)
    return (activations, feat_grad.astype(jnp.bfloat16), weight_grad)


def solution(mesh):
    placed = (
        P("blk", None),
        P(),
        P("blk", "rep", None, None, None, None),
        P("blk", "rep", None, None),
        P("blk", "rep", None),
        P(("blk", "rep"), None),
    )
    return jax.shard_map(
        local,
        mesh=mesh,
        in_specs=placed,
        out_specs=(P(("blk", "rep"), None), P(("blk", "rep"), None), P()),
        check_vma=False,
    )
```

profile of v0, /device:TPU:1, one launch (start us, length us, event | category | flops | bytes accessed | tf_op | source)
XLA Modules:
  0.0 915.5 jit_solution(509710526468673986)
XLA Ops:
  7.2 1.8 collective-permute-start
  9.0 0.7 copy-done.3
  9.8 0.8 copy.13
  10.6 0.7 iota_compare_fusion.1
  11.2 0.7 iota_reduce_fusion
  11.9 0.6 gather_fusion.1
  12.5 0.1 reshape.130
  12.6 0.1 fusion.13
  12.7 0.6 gather_fusion
  13.3 0.1 copy.14
  13.4 0.1 copy.15
  13.5 3.1 gather_fusion.2
  16.6 3.9 fusion
  20.5 2.3 copy.16
  22.7 72.2 %all-gather.3.cloned.1.call-done = bf16[4096,128]{1,0:T(8,128)(2,1)} async-done(((bf16[512,128]{1,0:T(8,128)(2,1)}), bf16[4096,128]{1,0:T(8,128)(2,1)}) %all-gather.3.cloned.1.call-update) | async-done | bytes 1048592 | tf_op jit(solution)/shard_map/all_gather | solution.py:53
  94.9 4.4 convolution_bitcast_fusion.1
  99.5 6.5 copy.17
  105.9 29.8 %reduce-scatter.4.cloned.1.call-done = f32[64,128]{1,0:T(8,128)} async-done(((f32[512,128]{1,0:T(8,128)}), f32[64,128]{1,0:T(8,128)}) %reduce-scatter.4.cloned.1.call-update) | async-done | bytes 32784 | tf_op jit(solution)/shard_map/reduce_scatter | solution.py:58
  135.7 0.9 fusion.25
  136.6 1.6 fusion.4
  138.3 0.1 convolution_convert_fusion
  138.4 21.9 %all_gather.11 = bf16[512,128]{1,0:T(8,128)(2,1)S(1)} all-gather(bf16[64,128]{1,0:T(8,128)(2,1)S(1)} %convolution_convert_fusion), channel_id=1, replica_groups=mesh['blk'=64,'rep'=8] {'rep'}, dimensions={0}, use_global_device_ids=true | all-gather | bytes 147456 | tf_op jit(solution)/shard_map/all_gather | solution.py:73
  160.3 4.8 convolution_bitcast_fusion
  165.2 112.6 %reduce-scatter.6.cloned.1.call-done = f32[1,512,128]{2,1,0:T(8,128)} async-done(((f32[8,512,128]{2,1,0:T(8,128)}), f32[1,512,128]{2,1,0:T(8,128)}) %reduce-scatter.6.cloned.1.call-update) | async-done | bytes 262160 | tf_op jit(solution)/shard_map/reduce_scatter | solution.py:77
  277.8 1.6 collective-permute-start.1
  279.4 0.9 fusion.22
  280.3 0.7 copy-done.2
  281.1 80.8 %all-reduce.3.cloned.1.call-done = f32[128,256]{1,0:T(8,128)} async-done(((f32[128,256]{1,0:T(8,128)}), f32[128,256]{1,0:T(8,128)}) %all-reduce.3.cloned.1.call-update) | async-done | bytes 131088 | tf_op jit(solution)/shard_map/psum | solution.py:69
  361.9 45.1 %reduce-scatter.8.cloned.1.call-done = f32[64,128]{1,0:T(8,128)} async-done(((f32[512,128]{1,0:T(8,128)}), f32[64,128]{1,0:T(8,128)}) %reduce-scatter.8.cloned.1.call-update) | async-done | bytes 32784 | tf_op jit(solution)/shard_map/reduce_scatter | solution.py:79
  407.0 1.4 convert_element_type.32
  408.4 498.8 %all-reduce.5.cloned.1.call-done = f32[128,256]{1,0:T(8,128)} async-done(((f32[128,256]{1,0:T(8,128)}), f32[128,256]{1,0:T(8,128)}) %all-reduce.5.cloned.1.call-update) | async-done | bytes 131088 | tf_op jit(solution)/shard_map/psum | solution.py:69
  907.1 1.6 copy.22
  (28 shorter events, 0.5 us)
Async XLA Ops:
  7.2 6.3 copy-start
  7.2 87.7 %all-gather.3.cloned.1.call-start = ((), (), s32[]{:S(2)}) async-start(), calls=%async_computation.8 | async-start | bytes 1179648 | tf_op jit(solution)/shard_map/all_gather | solution.py:53
  7.2 1.8 collective-permute-start
  9.0 0.7 copy-start.3
  9.7 126.0 %reduce-scatter.4.cloned.1.call-start = ((), (), s32[]{:S(2)}) async-start(), calls=%async_computation.3 | async-start | bytes 294912 | tf_op jit(solution)/shard_map/reduce_scatter | solution.py:58
  99.4 178.4 %reduce-scatter.6.cloned.1.call-start = ((), (), s32[]{:S(2)}) async-start(), calls=%async_computation.4 | async-start | bytes 2359296 | tf_op jit(solution)/shard_map/reduce_scatter | solution.py:77
  99.4 36.3 %copy-start.1 = (bf16[128,256]{1,0:T(8,128)(2,1)S(1)}, bf16[128,256]{1,0:T(8,128)(2,1)}, u32[]{:S(2)}) copy-start(bf16[128,256]{1,0:T(8,128)(2,1)} %param.7) | copy-start | bytes 196612
  99.4 37.2 %copy-start.5 = (bf16[64,256]{1,0:T(8,128)(2,1)S(1)}, bf16[64,256]{1,0:T(8,128)(2,1)}, u32[]{:S(2)}) copy-start(bf16[64,256]{1,0:T(8,128)(2,1)} %param.11) | copy-start | bytes 98308
  160.3 119.0 %copy-start.4 = (f32[64,128]{1,0:T(8,128)S(1)}, f32[64,128]{1,0:T(8,128)}, u32[]{:S(2)}) copy-start(f32[64,128]{1,0:T(8,128)} %reduce-scatter.4.cloned.1.call-done) | copy-start | bytes 98308
  165.2 196.7 %all-reduce.3.cloned.1.call-start = ((), (), s32[]{:S(2)}) async-start(), calls=%async_computation.6 | async-start | bytes 262144 | tf_op jit(solution)/shard_map/psum | solution.py:69
  277.8 2.5 collective-permute-start.1
  280.2 126.8 %reduce-scatter.8.cloned.1.call-start = ((), (), s32[]{:S(2)}) async-start(), calls=%async_computation.5 | async-start | bytes 294912 | tf_op jit(solution)/shard_map/reduce_scatter | solution.py:79
  280.3 0.7 copy-start.2
  281.0 626.1 %all-reduce.5.cloned.1.call-start = ((), (), s32[]{:S(2)}) async-start(), calls=%async_computation.7 | async-start | bytes 262144 | tf_op jit(solution)/shard_map/psum | solution.py:69
Sparse Core Ops, SparseCore 0:
  11.8 83.0 all-gather.2
  99.5 36.1 reduce-scatter.3
  165.3 112.4 reduce-scatter.5
  281.1 80.7 all-reduce.2
  364.5 42.4 reduce-scatter.7
  409.8 497.3 all-reduce.4
where the time goes:
time: 916 us
  waiting for transfers between devices  839 us (92%)
  blocking collectives  21.9 us (2%)
  local copies, waits for them, and re-layouts  17 us (2%)
  between operations  14.2 us (2%)
  matrix products  12.8 us (1%)
    psum x2, waiting for transfers between devices, local(): weight_grad = lax.psum(lax.psum(weight_grad, 'rep'), 'blk')  580 us
    reduce_scatter x1, waiting for transfers between devices, local(): lax.psum_scatter(partial, 'blk', scatter_dimension=0, axis_index_groups=r...  113 us
    all_gather x1, waiting for transfers between devices, local(): lax.all_gather(skewed(features, 1), 'blk', axis_index_groups=rings)  72.2 us
    reduce_scatter x1, waiting for transfers between devices, local(): lax.psum_scatter(partial, 'rep', scatter_dimension=0, tiled=True)  45.1 us
    reduce_scatter x1, waiting for transfers between devices, local(): mixed = lax.psum_scatter(mixed, 'rep', scatter_dimension=0, tiled=True)  29.8 us
    all_gather x1, blocking collectives, local(): lax.all_gather(row_grad, 'rep', axis=0, tiled=True)  21.9 us
  transfers between devices with their start and end apart: 8, of which 6 were waited for; matrix products, arithmetic and copies ran while one was open for 2% of the time, Pallas kernels for 0%

commit v1 on v0

--- a/solution.py
+++ b/solution.py
@@ -1,7 +1,22 @@
+import functools
 import jax
 import jax.numpy as jnp
 from jax import lax
 from jax.sharding import PartitionSpec as P
+
+
+def open_region_all(local_block, shard_axis):
+    frame_out = lax.all_to_all(
+        jnp.stack([local_block] * lax.axis_size(shard_axis)),
+        axis_name=shard_axis,
+        split_axis=0,
+        concat_axis=0,
+    )
+    w1 = jnp.concatenate(frame_out, axis=0)
+    return w1
+
+
+prepare_meshes_for = functools.partial(open_region_all, shard_axis="rep")
 
 
 def gelu_tanh(value):
@@ -70,7 +85,7 @@
     row_grad = lax.dot_general(
         pre_grad, weight, (((1,), (1,)), ((), ())), preferred_element_type=jnp.float32
     ).astype(jnp.bfloat16)
-    row_grad = lax.all_gather(row_grad, "rep", axis=0, tiled=True).reshape(blocks, tile_size, feat)
+    row_grad = prepare_meshes_for(row_grad).reshape(blocks, tile_size, feat)
     partial = jnp.einsum(
         "jnmik,nif->jmkf", adjacency, row_grad, preferred_element_type=jnp.float32
     ).reshape(-1, rows, feat)

time: 916 us -> 900 us (0.983)
  blocking collectives: 21.9 us -> 0 us
    all_gather x1 -> x0, blocking collectives: 21.9 us -> none  [local(): lax.all_gather(row_grad, 'rep', axis=0, tiled=True)]
  transfers between devices with their start and end apart: 8 -> 9, of which waited for: 6 -> 6; matrix products, arithmetic and copies ran while one was open for 2% -> 2% of each run, Pallas kernels for 0% -> 0%
where the time goes in v1:
time: 900 us
  waiting for transfers between devices  841 us (93%)
  local copies, waits for them, and re-layouts  17.7 us (2%)
  between operations  14.2 us (2%)
  matrix products  12.7 us (1%)
    psum x2, waiting for transfers between devices, local(): weight_grad = lax.psum(lax.psum(weight_grad, 'rep'), 'blk')  579 us
    reduce_scatter x1, waiting for transfers between devices, local(): lax.psum_scatter(partial, 'blk', scatter_dimension=0, axis_index_groups=r...  108 us
    all_gather x1, waiting for transfers between devices, local(): lax.all_gather(skewed(features, 1), 'blk', axis_index_groups=rings)  72.2 us
    reduce_scatter x1, waiting for transfers between devices, local(): lax.psum_scatter(partial, 'rep', scatter_dimension=0, tiled=True)  45.1 us
    reduce_scatter x1, waiting for transfers between devices, local(): mixed = lax.psum_scatter(mixed, 'rep', scatter_dimension=0, tiled=True)  36.4 us
  transfers between devices with their start and end apart: 9, of which 6 were waited for; matrix products, arithmetic and copies ran while one was open for 2% of the time, Pallas kernels for 0%

profile of v1, /device:TPU:1, one launch (start us, length us, event | category | flops | bytes accessed | tf_op | source)
XLA Modules:
  0.0 899.5 jit_solution(6040555237820607740)
XLA Ops:
  7.2 1.8 collective-permute-start
  9.0 0.7 copy-done.3
  9.8 0.8 copy.13
  10.6 0.7 iota_compare_fusion.1
  11.2 0.7 iota_reduce_fusion
  11.9 0.6 gather_fusion.1
  12.6 0.1 fusion.13
  12.7 0.6 gather_fusion
  13.3 0.1 copy.14
  13.4 0.1 copy.15
  13.5 3.1 gather_fusion.2
  16.6 3.9 fusion
  20.5 2.3 copy.16
  22.7 72.2 %all-gather.3.cloned.1.call-done = bf16[4096,128]{1,0:T(8,128)(2,1)} async-done(((bf16[512,128]{1,0:T(8,128)(2,1)}), bf16[4096,128]{1,0:T(8,128)(2,1)}) %all-gather.3.cloned.1.call-update) | async-done | bytes 1048592 | tf_op jit(solution)/shard_map/all_gather | solution.py:68
  94.9 4.4 convolution_bitcast_fusion.1
  99.4 36.4 %reduce-scatter.4.cloned.1.call-done = f32[64,128]{1,0:T(8,128)} async-done(((f32[512,128]{1,0:T(8,128)}), f32[64,128]{1,0:T(8,128)}) %reduce-scatter.4.cloned.1.call-update) | async-done | bytes 32784 | tf_op jit(solution)/shard_map/reduce_scatter | solution.py:73
  135.7 0.9 fusion.25
  136.6 1.6 fusion.4
  138.3 0.1 convolution_convert_fusion
  138.4 0.7 stack.2
  139.1 3.4 all-to-all-start
  142.5 6.5 copy.17
  149.0 4.8 convolution_bitcast_fusion
  153.9 108.0 %reduce-scatter.6.cloned.1.call-done = f32[1,512,128]{2,1,0:T(8,128)} async-done(((f32[8,512,128]{2,1,0:T(8,128)}), f32[1,512,128]{2,1,0:T(8,128)}) %reduce-scatter.6.cloned.1.call-update) | async-done | bytes 262160 | tf_op jit(solution)/shard_map/reduce_scatter | solution.py:92
  261.9 1.6 collective-permute-start.1
  263.5 0.9 fusion.22
  264.4 0.7 copy-done.2
  265.2 80.7 %all-reduce.3.cloned.1.call-done = f32[128,256]{1,0:T(8,128)} async-done(((f32[128,256]{1,0:T(8,128)}), f32[128,256]{1,0:T(8,128)}) %all-reduce.3.cloned.1.call-update) | async-done | bytes 131088 | tf_op jit(solution)/shard_map/psum | solution.py:84
  345.9 45.1 %reduce-scatter.8.cloned.1.call-done = f32[64,128]{1,0:T(8,128)} async-done(((f32[512,128]{1,0:T(8,128)}), f32[64,128]{1,0:T(8,128)}) %reduce-scatter.8.cloned.1.call-update) | async-done | bytes 32784 | tf_op jit(solution)/shard_map/reduce_scatter | solution.py:94
  391.0 1.4 convert_element_type.32
  392.4 498.8 %all-reduce.5.cloned.1.call-done = f32[128,256]{1,0:T(8,128)} async-done(((f32[128,256]{1,0:T(8,128)}), f32[128,256]{1,0:T(8,128)}) %all-reduce.5.cloned.1.call-update) | async-done | bytes 131088 | tf_op jit(solution)/shard_map/psum | solution.py:84
  891.1 1.6 copy.22
  (30 shorter events, 0.6 us)
Async XLA Ops:
  7.2 6.3 copy-start
  7.2 87.7 %all-gather.3.cloned.1.call-start = ((), (), s32[]{:S(2)}) async-start(), calls=%async_computation.9 | async-start | bytes 1179648 | tf_op jit(solution)/shard_map/all_gather | solution.py:68
  7.2 1.8 collective-permute-start
  9.0 0.7 copy-start.3
  9.7 126.0 %reduce-scatter.4.cloned.1.call-start = ((), (), s32[]{:S(2)}) async-start(), calls=%async_computation.4 | async-start | bytes 294912 | tf_op jit(solution)/shard_map/reduce_scatter | solution.py:73
  22.7 113.0 %copy-start.1 = (bf16[128,256]{1,0:T(8,128)(2,1)S(1)}, bf16[128,256]{1,0:T(8,128)(2,1)}, u32[]{:S(2)}) copy-start(bf16[128,256]{1,0:T(8,128)(2,1)} %param.7) | copy-start | bytes 196612
  22.7 113.9 %copy-start.5 = (bf16[64,256]{1,0:T(8,128)(2,1)S(1)}, bf16[64,256]{1,0:T(8,128)(2,1)}, u32[]{:S(2)}) copy-start(bf16[64,256]{1,0:T(8,128)(2,1)} %param.11) | copy-start | bytes 98308
  139.1 9.9 %all-to-all-start = ((bf16[8,64,128]{2,1,0:T(8,128)(2,1)}), bf16[8,64,128]{2,1,0:T(8,128)(2,1)S(1)}, u32[]{:S(2)}, u32[]{:S(2)}) async-start(bf16[8,64,128]{2,1,0:T(8,128)(2,1)} %stack.2), calls=%async_computation.1 | async-start | bytes 262144 | tf_op jit(solution)/shard_map/all_to_all | solution.py:9
  142.5 119.4 %reduce-scatter.6.cloned.1.call-start = ((), (), s32[]{:S(2)}) async-start(), calls=%async_computation.5 | async-start | bytes 2359296 | tf_op jit(solution)/shard_map/reduce_scatter | solution.py:92
  149.0 114.4 %copy-start.4 = (f32[64,128]{1,0:T(8,128)S(1)}, f32[64,128]{1,0:T(8,128)}, u32[]{:S(2)}) copy-start(f32[64,128]{1,0:T(8,128)} %reduce-scatter.4.cloned.1.call-done) | copy-start | bytes 98308
  153.9 192.0 %all-reduce.3.cloned.1.call-start = ((), (), s32[]{:S(2)}) async-start(), calls=%async_computation.7 | async-start | bytes 262144 | tf_op jit(solution)/shard_map/psum | solution.py:84
  261.9 2.5 collective-permute-start.1
  264.4 126.6 %reduce-scatter.8.cloned.1.call-start = ((), (), s32[]{:S(2)}) async-start(), calls=%async_computation.6 | async-start | bytes 294912 | tf_op jit(solution)/shard_map/reduce_scatter | solution.py:94
  264.4 0.7 copy-start.2
  265.1 626.0 %all-reduce.5.cloned.1.call-start = ((), (), s32[]{:S(2)}) async-start(), calls=%async_computation.8 | async-start | bytes 262144 | tf_op jit(solution)/shard_map/psum | solution.py:84
Sparse Core Ops, SparseCore 0:
  11.8 83.0 all-gather.2
  99.5 36.1 reduce-scatter.3
  154.0 107.8 reduce-scatter.5
  265.2 80.6 all-reduce.2
  348.5 42.4 reduce-scatter.7
  393.8 497.3 all-reduce.4

commit v2 on v0

--- a/solution.py
+++ b/solution.py
@@ -66,7 +66,12 @@
         (((0,), (0,)), ((), ())),
         preferred_element_type=jnp.float32,
     )
-    weight_grad = lax.psum(lax.psum(weight_grad, "rep"), "blk")
+
+    def link_shelves(here_x):
+        reply = lax.all_gather(here_x, "rep").sum(axis=0)
+        return reply
+
+    weight_grad = lax.psum(link_shelves(weight_grad), "blk")
     row_grad = lax.dot_general(
         pre_grad, weight, (((1,), (1,)), ((), ())), preferred_element_type=jnp.float32
     ).astype(jnp.bfloat16)

time: 916 us -> 872 us (0.952)
  waiting for transfers between devices: 839 us -> 793 us
    psum x2 -> x1, waiting for transfers between devices: 580 us -> 499 us  [local(): weight_grad = lax.psum(link_shelves(weight_grad), 'blk')]
    all_gather x0 -> x1, waiting for transfers between devices: none -> 37.6 us  [link_shelves(): reply = lax.all_gather(here_x, 'rep').sum(axis=0)]
  transfers between devices with their start and end apart: 8 -> 8, of which waited for: 6 -> 6; matrix products, arithmetic and copies ran while one was open for 2% -> 3% of each run, Pallas kernels for 0% -> 0%
where the time goes in v2:
time: 872 us
  waiting for transfers between devices  793 us (91%)
  blocking collectives  21.9 us (3%)
  local copies, waits for them, and re-layouts  17 us (2%)
  between operations  14.2 us (2%)
  matrix products  12.8 us (1%)
    psum x1, waiting for transfers between devices, local(): weight_grad = lax.psum(link_shelves(weight_grad), 'blk')  499 us
    reduce_scatter x1, waiting for transfers between devices, local(): lax.psum_scatter(partial, 'blk', scatter_dimension=0, axis_index_groups=r...  111 us
    all_gather x1, waiting for transfers between devices, local(): lax.all_gather(skewed(features, 1), 'blk', axis_index_groups=rings)  72.2 us
    reduce_scatter x1, waiting for transfers between devices, local(): lax.psum_scatter(partial, 'rep', scatter_dimension=0, tiled=True)  43 us
    all_gather x1, waiting for transfers between devices, link_shelves(): reply = lax.all_gather(here_x, 'rep').sum(axis=0)  37.6 us
    reduce_scatter x1, waiting for transfers between devices, local(): mixed = lax.psum_scatter(mixed, 'rep', scatter_dimension=0, tiled=True)  29.8 us
    all_gather x1, blocking collectives, local(): lax.all_gather(row_grad, 'rep', axis=0, tiled=True)  21.9 us
  transfers between devices with their start and end apart: 8, of which 6 were waited for; matrix products, arithmetic and copies ran while one was open for 3% of the time, Pallas kernels for 0%

profile of v2, /device:TPU:1, one launch (start us, length us, event | category | flops | bytes accessed | tf_op | source)
XLA Modules:
  0.0 871.6 jit_solution(17729844135521476849)
XLA Ops:
  7.2 1.8 collective-permute-start
  9.0 0.7 copy-done.3
  9.8 0.8 copy.13
  10.6 0.7 iota_compare_fusion.1
  11.2 0.7 iota_reduce_fusion
  11.9 0.6 gather_fusion.1
  12.6 0.1 fusion.13
  12.7 0.6 gather_fusion
  13.3 0.1 copy.14
  13.4 0.1 copy.15
  13.5 3.1 gather_fusion.2
  16.6 3.9 fusion
  20.5 2.3 copy.16
  22.7 72.2 %all-gather.5.cloned.1.call-done = bf16[4096,128]{1,0:T(8,128)(2,1)} async-done(((bf16[512,128]{1,0:T(8,128)(2,1)}), bf16[4096,128]{1,0:T(8,128)(2,1)}) %all-gather.5.cloned.1.call-update) | async-done | bytes 1048592 | tf_op jit(solution)/shard_map/all_gather | solution.py:53
  94.9 4.4 convolution_bitcast_fusion.1
  99.5 6.5 copy.17
  105.9 29.8 %reduce-scatter.4.cloned.1.call-done = f32[64,128]{1,0:T(8,128)} async-done(((f32[512,128]{1,0:T(8,128)}), f32[64,128]{1,0:T(8,128)}) %reduce-scatter.4.cloned.1.call-update) | async-done | bytes 32784 | tf_op jit(solution)/shard_map/reduce_scatter | solution.py:58
  135.7 0.9 fusion.25
  136.6 1.6 fusion.4
  138.3 0.1 convolution_convert_fusion
  138.4 21.9 %all_gather.17 = bf16[512,128]{1,0:T(8,128)(2,1)S(1)} all-gather(bf16[64,128]{1,0:T(8,128)(2,1)S(1)} %convolution_convert_fusion), channel_id=1, replica_groups=mesh['blk'=64,'rep'=8] {'rep'}, dimensions={0}, use_global_device_ids=true | all-gather | bytes 147456 | tf_op jit(solution)/shard_map/all_gather | solution.py:78
  160.3 4.8 convolution_bitcast_fusion
  165.2 0.9 fusion.22
  166.2 111.4 %reduce-scatter.6.cloned.1.call-done = f32[1,512,128]{2,1,0:T(8,128)} async-done(((f32[8,512,128]{2,1,0:T(8,128)}), f32[1,512,128]{2,1,0:T(8,128)}) %reduce-scatter.6.cloned.1.call-update) | async-done | bytes 262160 | tf_op jit(solution)/shard_map/reduce_scatter | solution.py:82
  277.5 1.6 collective-permute-start.1
  279.1 0.7 copy-done.2
  279.9 37.6 %all-gather.7.cloned.1.call-done = f32[1024,256]{1,0:T(8,128)} async-done(((f32[128,256]{1,0:T(8,128)}), f32[1024,256]{1,0:T(8,128)}) %all-gather.7.cloned.1.call-update) | async-done | bytes 1048592 | tf_op jit(solution)/shard_map/all_gather | solution.py:71
  317.5 2.0 reduce_sum.9
  319.5 43.0 %reduce-scatter.8.cloned.1.call-done = f32[64,128]{1,0:T(8,128)} async-done(((f32[512,128]{1,0:T(8,128)}), f32[64,128]{1,0:T(8,128)}) %reduce-scatter.8.cloned.1.call-update) | async-done | bytes 32784 | tf_op jit(solution)/shard_map/reduce_scatter | solution.py:84
  362.4 1.4 convert_element_type.32
  363.8 499.4 %all-reduce.2.cloned.1.call-done = f32[128,256]{1,0:T(8,128)} async-done(((f32[128,256]{1,0:T(8,128)}), f32[128,256]{1,0:T(8,128)}) %all-reduce.2.cloned.1.call-update) | async-done | bytes 131088 | tf_op jit(solution)/shard_map/psum | solution.py:74
  863.2 1.6 copy.21
  (29 shorter events, 0.6 us)
Async XLA Ops:
  7.2 6.3 copy-start
  7.2 87.7 %all-gather.5.cloned.1.call-start = ((), (), s32[]{:S(2)}) async-start(), calls=%async_computation.7 | async-start | bytes 1179648 | tf_op jit(solution)/shard_map/all_gather | solution.py:53
  7.2 1.8 collective-permute-start
  9.0 0.7 copy-start.3
  9.7 126.0 %reduce-scatter.4.cloned.1.call-start = ((), (), s32[]{:S(2)}) async-start(), calls=%async_computation.3 | async-start | bytes 294912 | tf_op jit(solution)/shard_map/reduce_scatter | solution.py:58
  99.4 178.1 %reduce-scatter.6.cloned.1.call-start = ((), (), s32[]{:S(2)}) async-start(), calls=%async_computation.4 | async-start | bytes 2359296 | tf_op jit(solution)/shard_map/reduce_scatter | solution.py:82
  99.4 36.3 %copy-start.1 = (bf16[128,256]{1,0:T(8,128)(2,1)S(1)}, bf16[128,256]{1,0:T(8,128)(2,1)}, u32[]{:S(2)}) copy-start(bf16[128,256]{1,0:T(8,128)(2,1)} %param.7) | copy-start | bytes 196612
  99.4 37.2 %copy-start.5 = (bf16[64,256]{1,0:T(8,128)(2,1)S(1)}, bf16[64,256]{1,0:T(8,128)(2,1)}, u32[]{:S(2)}) copy-start(bf16[64,256]{1,0:T(8,128)(2,1)} %param.11) | copy-start | bytes 98308
  160.3 4.9 copy-start.4
  165.2 152.3 %all-gather.7.cloned.1.call-start = ((), (), s32[]{:S(2)}) async-start(), calls=%async_computation.8 | async-start | bytes 1179648 | tf_op jit(solution)/shard_map/all_gather | solution.py:71
  166.1 196.3 %reduce-scatter.8.cloned.1.call-start = ((), (), s32[]{:S(2)}) async-start(), calls=%async_computation.5 | async-start | bytes 294912 | tf_op jit(solution)/shard_map/reduce_scatter | solution.py:84
  277.5 1.6 collective-permute-start.1
  279.1 0.7 copy-start.2
  279.8 583.4 %all-reduce.2.cloned.1.call-start = ((), (), s32[]{:S(2)}) async-start(), calls=%async_computation.6 | async-start | bytes 262144 | tf_op jit(solution)/shard_map/psum | solution.py:74
Sparse Core Ops, SparseCore 0:
  11.8 83.0 all-gather.4
  99.5 36.1 reduce-scatter.3
  165.3 112.1 reduce-scatter.5
  280.0 37.4 all-gather.6
  320.1 42.2 reduce-scatter.7
  365.8 497.3 all-reduce.1
